TPU v7x, 32 devices: a whole 2x2x4 slice. The times are simulated.
32 devices in a mesh: dp: 16 (over z, y, core), own: 2 (over x).
Axes of the slice: x: 2, y: 2, z: 4, core: 2. Of those that a mesh axis runs over, the one named last changes fastest.
Arguments:
- layer_inputs: bfloat16 [4, 16, 16, 128, 128], P(None, 'dp', 'own'), as said below
- weights: bfloat16 [4, 1152, 128], replicated, may hold values from -0.1875 to 0.1875
- top_cotangent: bfloat16 [16, 16, 128, 128], P('dp', 'own'), may hold values from -6 to 6
- segmentation: int32 [16, 16, 128], P('dp', 'own'), may hold values from 0 to 2
- layer_slots: int32 [4], replicated, may hold values from 0 to 3, as said below
- a_inverse: bfloat16 [4, 1152, 1152], P('own', 'dp'), as said below
- g_inverse: bfloat16 [4, 128, 128], P('own'), as said below
Outputs:
- preconditioned: float32 [4, 1152, 128], P(None, 'dp')
- input_grad: bfloat16 [16, 16, 128, 128], P('dp', 'own')
Inputs may be any that keep to these rules, and one draw needn't show every extreme that they name: Distinct slot numbers; layer l is held by owner layer_slots[l] // 2, in that owner's slot layer_slots[l] % 2. One owner holds exactly 2 layers in every draw. `a_inverse`: each factor is symmetric. `g_inverse`: each factor is symmetric. `layer_inputs`: activations after a rectifier.
All inputs are finite; a program needn't handle non-finite values.
Results may differ from a plain program's by a relative error of at most 0.011.
Values may be sent and summed in bfloat16 or wider, within the bound.
A program may use at most 64 MiB of HBM per device.

v0:
```python
import math
import jax
import jax.numpy as jnp
from jax import lax
from jax.sharding import PartitionSpec as P


def extended(cells, sides, width):
    for axis, dim in sides:
        count = lax.axis_size(axis)
        ends = count - 1
        head = lax.slice_in_dim(cells, 0, width, axis=dim)
        tail = lax.slice_in_dim(cells, cells.shape[dim] - width, cells.shape[dim], axis=dim)
        cells = jnp.concatenate(
            [
                lax.ppermute(tail, axis, [(i, (i + 1) % count) for i in range(ends)]),
                cells,
                lax.ppermute(head, axis, [((i + 1) % count, i) for i in range(ends)]),
            ],
            axis=dim,
        )
    return cells


def from_root(block, axis, owner):
    block = jnp.where(lax.axis_index(axis) == owner, block, jnp.zeros_like(block))
    return lax.psum(block, axis)


def loss_weight(labels):
    return jnp.where(labels == 0, 1.0, jnp.where(labels == 1, 0.0, 0.5)).astype(jnp.float32)


def tap_matrix(padded, num_rows, num_cols):
    channels = padded.shape[-1]
    pieces = []
    for tap_index in range(9):
        row_start = 2 - tap_index // 3
        col_start = 2 - tap_index % 3
        pieces.append(padded[row_start : row_start + num_rows, col_start : col_start + num_cols])
    stacked = jnp.stack(pieces, axis=2)
    return stacked.reshape(num_rows * num_cols, 9 * channels)


def per_device(
    layer_inputs, weights, top_cotangent, segmentation, layer_slots, a_inverse, g_inverse
):
    layer_count = layer_inputs.shape[0]
    num_rows = layer_inputs.shape[2]
    num_cols = layer_inputs.shape[3]
    channels = layer_inputs.shape[4]
    data_devices = lax.axis_size("dp")
    owner_devices = lax.axis_size("own")
    grad_scale = 1.0 / math.sqrt(data_devices * owner_devices * num_rows * num_cols)
    inputs_local = layer_inputs[:, 0]
    scaled = loss_weight(segmentation[0])[:, :, None] * top_cotangent[0].astype(jnp.float32)
    out_grad = scaled.astype(jnp.bfloat16)
    grad_blocks = [None] * layer_count
    input_grad = None
    for layer_index in range(layer_count - 1, -1, -1):
        rimmed = extended(out_grad, (("own", 0),), 1)
        padded = jnp.pad(rimmed, ((0, 0), (1, 1), (0, 0)))
        tap_rows = tap_matrix(padded, num_rows, num_cols)
        flat_inputs = inputs_local[layer_index].reshape(num_rows * num_cols, channels)
        grad_block = lax.dot_general(
            flat_inputs, tap_rows, (((0,), (0,)), ((), ())), preferred_element_type=jnp.float32
        )
        grad_blocks[layer_index] = grad_block.reshape(9 * channels, channels) * grad_scale
        kernel = weights[layer_index].reshape(channels, 9 * channels)
        input_side = lax.dot_general(
            tap_rows, kernel, (((1,), (1,)), ((), ())), preferred_element_type=jnp.float32
        )
        input_side = input_side.reshape(num_rows, num_cols, channels)
        if layer_index > 0:
            out_grad = jnp.where(inputs_local[layer_index] > 0, input_side, 0.0).astype(
                jnp.bfloat16
            )
        else:
            input_grad = input_side.astype(jnp.bfloat16)[None]
    grad_term = jnp.concatenate(grad_blocks, axis=1)
    grad_rows = lax.psum_scatter(grad_term, "dp", scatter_dimension=0, tiled=True)
    slot_count = a_inverse.shape[0]
    grad_sum = lax.psum(grad_rows.astype(jnp.bfloat16), "own")
    left_panels = []
    right_panels = []
    for layer_index in range(layer_count):
        slot_id = layer_slots[layer_index]
        owner_index = slot_id // slot_count
        local_slot = slot_id % slot_count
        left_panel = lax.dynamic_index_in_dim(a_inverse, local_slot, 0, keepdims=False)
        right_panel = lax.dynamic_index_in_dim(g_inverse, local_slot, 0, keepdims=False)
        left_panel, right_panel = (
            from_root(left_panel, "own", owner_index),
            from_root(right_panel, "own", owner_index),
        )
        left_panels.append(left_panel)
        right_panels.append(right_panel)
    left_stack = jnp.stack(left_panels, axis=0)
    right_stack = jnp.stack(right_panels, axis=0)
    gathered_piece = lax.all_gather(grad_sum, "dp", axis=0, tiled=True)
    width_here = gathered_piece.shape[0]
    shaped_piece = gathered_piece.reshape(width_here, layer_count, channels)
    left_product = jnp.einsum(
        "lrn,nlc->lrc", left_stack, shaped_piece, preferred_element_type=jnp.float32
    )
    preconditioned = jnp.einsum(
        "lrc,lcd->lrd",
        left_product.astype(jnp.bfloat16),
        right_stack,
        preferred_element_type=jnp.float32,
    )
    return (preconditioned, input_grad)


def solution(mesh):
    in_specs = (
        P(None, "dp", "own", None, None),
        P(),
        P("dp", "own", None, None),
        P("dp", "own", None),
        P(),
        P("own", "dp", None),
        P("own", None, None),
    )
    out_specs = (P(None, "dp", None), P("dp", "own", None, None))
    return jax.shard_map(
        per_device, mesh=mesh, in_specs=in_specs, out_specs=out_specs, check_vma=False
    )
```

profile of v0, /device:TPU:0, one launch (start us, length us, event | category | flops | bytes accessed | tf_op | source)
XLA Modules:
  0.0 266.4 jit_solution(8736624988374941266)
XLA Ops:
  9.2 1.3 collective-permute-start.1
  10.5 4.8 %collective-permute-start = (bf16[1,128,128]{1,2,0:T(8,128)(2,1)S(1)}, bf16[1,128,128]{1,2,0:T(8,128)(2,1)S(1)}, u32[]{:S(2)}, u32[]{:S(2)}) collective-permute-start(bf16[1,128,128]{1,2,0:T(8,128)(2,1)S(1)} %get-tuple-element.29), channel_id=1, source_target_pairs={{0,1},{2,3},{4,5},{6,7},{8,9},{10,11},{12,13},{14,15},{16,17},{18,... | collective-permute-start | bytes 98312 | tf_op jit(solution)/shard_map/ppermute | solution.py:16
  15.4 1.3 fusion.111
  21.5 1.6 copy.30
  23.1 1.8 fusion.13
  26.9 5.1 %collective-permute-start.2 = (bf16[1,128,128]{2,1,0:T(8,128)(2,1)}, bf16[1,128,128]{2,1,0:T(8,128)(2,1)S(1)}, u32[]{:S(2)}, u32[]{:S(2)}) collective-permute-start(bf16[1,128,128]{2,1,0:T(8,128)(2,1)} %get-tuple-element.27), channel_id=1, source_target_pairs={{0,1},{2,3},{4,5},{6,7},{8,9},{10,11},{12,13},{14,15},{16,17},{18,... | collective-permute-start | bytes 98312 | tf_op jit(solution)/shard_map/ppermute | solution.py:16
  36.1 2.7 copy.28
  38.8 2.5 copy.20
  41.2 2.7 %fusion.14 = bf16[8,128,128]{2,1,0:T(8,128)(2,1)S(1)} fusion(bf16[8,128,1152]{1,2,0:T(8,128)(2,1)} %bitcast.255, bf16[128,1152,1]{1,0,2:T(8,128)(2,1)} %reshape.135, bf16[4,1,8,128,128]{4,3,2,1,0:T(8,128)(2,1)} %param.7), kind=kOutput, calls=%fused_computation.24 | convolution fusion | flops 302383104 | bytes 3178496 | tf_op jit(solution)/shard_map/dot_general | solution.py:70
  44.6 1.3 collective-permute-start.5
  45.9 5.3 %collective-permute-start.4 = (bf16[1,128,128]{2,1,0:T(8,128)(2,1)}, bf16[1,128,128]{2,1,0:T(8,128)(2,1)S(1)}, u32[]{:S(2)}, u32[]{:S(2)}) collective-permute-start(bf16[1,128,128]{2,1,0:T(8,128)(2,1)} %get-tuple-element.25), channel_id=1, source_target_pairs={{0,1},{2,3},{4,5},{6,7},{8,9},{10,11},{12,13},{14,15},{16,17},{18,... | collective-permute-start | bytes 98312 | tf_op jit(solution)/shard_map/ppermute | solution.py:16
  51.2 1.6 fusion.2
  52.8 1.3 copy.29
  57.2 2.7 copy.26
  59.9 2.5 copy.22
  62.3 2.7 %fusion.15 = bf16[8,128,128]{2,1,0:T(8,128)(2,1)S(1)} fusion(bf16[8,128,1152]{1,2,0:T(8,128)(2,1)} %bitcast.256, bf16[128,1152,1]{1,0,2:T(8,128)(2,1)} %reshape.136, bf16[4,1,8,128,128]{4,3,2,1,0:T(8,128)(2,1)} %param.7), kind=kOutput, calls=%fused_computation.25 | convolution fusion | flops 302383104 | bytes 3178496 | tf_op jit(solution)/shard_map/dot_general | solution.py:70
  67.0 5.1 %collective-permute-start.6 = (bf16[1,128,128]{2,1,0:T(8,128)(2,1)}, bf16[1,128,128]{2,1,0:T(8,128)(2,1)S(1)}, u32[]{:S(2)}, u32[]{:S(2)}) collective-permute-start(bf16[1,128,128]{2,1,0:T(8,128)(2,1)} %get-tuple-element.23), channel_id=1, source_target_pairs={{0,1},{2,3},{4,5},{6,7},{8,9},{10,11},{12,13},{14,15},{16,17},{18,... | collective-permute-start | bytes 98312 | tf_op jit(solution)/shard_map/ppermute | solution.py:16
  72.2 1.6 fusion.1
  73.7 1.3 copy.27
  78.1 2.7 copy.24
  80.8 3.3 %fusion = f32[128,1152]{0,1:T(8,128)} fusion(bf16[1024,128]{1,0:T(8,128)(2,1)S(1)} %bitcast.258, bf16[144,8,8,128]{3,2,1,0:T(8,128)(2,1)} %bitcast.257), kind=kOutput, calls=%fused_computation.4 | convolution fusion | flops 302137344 | bytes 3211264 | tf_op jit(solution)/shard_map/dot_general | solution.py:65
  84.0 2.1 copy.25
  86.2 1.9 mul.59
  88.1 3.0 %pad_maximum_fusion = f32[1152,512]{1,0:T(8,128)} fusion(f32[1152,128]{1,0:T(8,128)S(1)} %mul.68, f32[1152,128]{1,0:T(8,128)} %mul.65, f32[1152,128]{1,0:T(8,128)} %mul.62, f32[1152,128]{1,0:T(8,128)} %mul.59), kind=kLoop, calls=%fused_computation.16 | loop fusion | flops 1769472 | bytes 4718592 | tf_op jit(solution)/shard_map/concatenate | solution.py:80
  103.5 52.2 %reduce-scatter.2.cloned.1.call-done = f32[72,512]{1,0:T(8,128)} async-done(((f32[1152,512]{1,0:T(8,128)}), f32[72,512]{1,0:T(8,128)}) %reduce-scatter.2.cloned.1.call-update) | async-done | bytes 147472 | tf_op jit(solution)/shard_map/reduce_scatter | solution.py:81
  155.7 1.6 convert_element_type.58
  158.1 34.0 %all-reduce.11.cloned.1.call-done = (bf16[72,512]{1,0:T(8,128)(2,1)}, bf16[1,72,1152]{2,1,0:T(8,128)(2,1)}, bf16[1,72,1152]{2,1,0:T(8,128)(2,1)}, bf16[1,72,1152]{2,1,0:T(8,128)(2,1)}, bf16[1,72,1152]{2,1,0:T(8,128)(2,1)}) async-done(((bf16[72,512]{1,0:T(8,128)(2,1)}, bf16[1,72,1152]{2,1,0:T(8,128)(2,1)}, bf16[1,72,1152]{2,1,0:T(8,128)(2,1)}, bf16[1,72,1152]{2,1,0:T(8,128)(2,1)}, ...) | async-done | bytes 737296 | tf_op jit(solution)/shard_map/psum | solution.py:83
  192.4 2.5 copy.32
  194.9 3.3 %fusion.19 = bf16[1,8,128,128]{3,2,1,0:T(8,128)(2,1)} fusion(bf16[8,128,1152]{1,2,0:T(8,128)(2,1)} %bitcast.250, bf16[128,1152,1]{1,0,2:T(8,128)(2,1)S(1)} %reshape.137), kind=kOutput, calls=%fused_computation.30 | convolution fusion | flops 302120960 | bytes 2916352 | tf_op jit(solution)/shard_map/dot_general | solution.py:70
  198.2 18.3 %all-reduce.9.cloned.1.call-done = (bf16[1,128,128]{2,1,0:T(8,128)(2,1)}, bf16[1,128,128]{2,1,0:T(8,128)(2,1)}, bf16[1,128,128]{2,1,0:T(8,128)(2,1)}, bf16[1,128,128]{2,1,0:T(8,128)(2,1)}) async-done(((bf16[1,128,128]{2,1,0:T(8,128)(2,1)}, bf16[1,128,128]{2,1,0:T(8,128)(2,1)}, bf16[1,128,128]{2,1,0:T(8,128)(2,1)}, bf16[1,128,128]{2,1,0:T(8,128)(2,1)}), (bf16[1,128,128]{2,1,0:T(8,128)(2,1)}, ...) | async-done | bytes 131088 | tf_op jit(solution)/shard_map/psum | solution.py:27
  216.5 40.8 %all-gather.2.cloned.1.call-done = bf16[1152,512]{1,0:T(8,128)(2,1)} async-done(((bf16[72,512]{1,0:T(8,128)(2,1)}), bf16[1152,512]{1,0:T(8,128)(2,1)}) %all-gather.2.cloned.1.call-update) | async-done | bytes 1179664 | tf_op jit(solution)/shard_map/all_gather | solution.py:100
  257.3 2.5 fusion.24
  (106 shorter events, 24.5 us)
Async XLA Ops:
  7.2 9.5 %copy-start.3 = (bf16[4,1,8,128,128]{4,3,2,1,0:T(8,128)(2,1)S(1)}, bf16[4,1,8,128,128]{4,3,2,1,0:T(8,128)(2,1)}, u32[]{:S(2)}) copy-start(bf16[4,1,8,128,128]{4,3,2,1,0:T(8,128)(2,1)} %param.7) | copy-start | bytes 3145732
  7.2 148.5 %reduce-scatter.2.cloned.1.call-start = ((), (), s32[]{:S(2)}) async-start(), calls=%async_computation.1 | async-start | bytes 2506752 | tf_op jit(solution)/shard_map/reduce_scatter | solution.py:81
  9.2 11.0 %collective-permute-start.1 = (bf16[1,128,128]{1,2,0:T(8,128)(2,1)S(1)}, bf16[1,128,128]{1,2,0:T(8,128)(2,1)S(1)}, u32[]{:S(2)}, u32[]{:S(2)}) collective-permute-start(bf16[1,128,128]{1,2,0:T(8,128)(2,1)S(1)} %get-tuple-element.30), channel_id=1, source_target_pairs={{1,0},{3,2},{5,4},{7,6},{9,8},{11,10},{13,12},{15,14},{17,16},{19,... | collective-permute-start | bytes 98312 | tf_op jit(solution)/shard_map/ppermute | solution.py:18
  10.5 9.7 %collective-permute-start = (bf16[1,128,128]{1,2,0:T(8,128)(2,1)S(1)}, bf16[1,128,128]{1,2,0:T(8,128)(2,1)S(1)}, u32[]{:S(2)}, u32[]{:S(2)}) collective-permute-start(bf16[1,128,128]{1,2,0:T(8,128)(2,1)S(1)} %get-tuple-element.29), channel_id=1, source_target_pairs={{0,1},{2,3},{4,5},{6,7},{8,9},{10,11},{12,13},{14,15},{16,17},{18,... | collective-permute-start | bytes 98312 | tf_op jit(solution)/shard_map/ppermute | solution.py:16
  23.1 8.9 %copy-start.8 = (bf16[1,1,8,128,128]{4,3,2,1,0:T(8,128)(2,1)S(1)}, bf16[1,1,8,128,128]{4,3,2,1,0:T(8,128)(2,1)}, u32[]{:S(2)}) copy-start(bf16[1,1,8,128,128]{4,3,2,1,0:T(8,128)(2,1)} %get-tuple-element.18) | copy-start | bytes 786436
  25.6 7.5 %collective-permute-start.3 = (bf16[1,128,128]{2,1,0:T(8,128)(2,1)}, bf16[1,128,128]{2,1,0:T(8,128)(2,1)}, u32[]{:S(2)}, u32[]{:S(2)}) collective-permute-start(bf16[1,128,128]{2,1,0:T(8,128)(2,1)} %get-tuple-element.28), channel_id=1, source_target_pairs={{1,0},{3,2},{5,4},{7,6},{9,8},{11,10},{13,12},{15,14},{17,16},{19,... | collective-permute-start | bytes 98312 | tf_op jit(solution)/shard_map/ppermute | solution.py:18
  26.9 7.0 %collective-permute-start.2 = (bf16[1,128,128]{2,1,0:T(8,128)(2,1)}, bf16[1,128,128]{2,1,0:T(8,128)(2,1)S(1)}, u32[]{:S(2)}, u32[]{:S(2)}) collective-permute-start(bf16[1,128,128]{2,1,0:T(8,128)(2,1)} %get-tuple-element.27), channel_id=1, source_target_pairs={{0,1},{2,3},{4,5},{6,7},{8,9},{10,11},{12,13},{14,15},{16,17},{18,... | collective-permute-start | bytes 98312 | tf_op jit(solution)/shard_map/ppermute | solution.py:16
  41.2 10.0 %copy-start = (bf16[8,128,9,128]{1,0,3,2:T(8,128)(2,1)S(1)}, bf16[8,128,9,128]{1,0,3,2:T(8,128)(2,1)}, u32[]{:S(2)}) copy-start(bf16[8,128,9,128]{1,0,3,2:T(8,128)(2,1)} %copy.28) | copy-start | bytes 7077892
  41.2 10.0 %copy-start.7 = (bf16[1,1,8,128,128]{4,3,2,1,0:T(8,128)(2,1)S(1)}, bf16[1,1,8,128,128]{4,3,2,1,0:T(8,128)(2,1)}, u32[]{:S(2)}) copy-start(bf16[1,1,8,128,128]{4,3,2,1,0:T(8,128)(2,1)} %get-tuple-element.16) | copy-start | bytes 786436
  44.6 10.4 %collective-permute-start.5 = (bf16[1,128,128]{2,1,0:T(8,128)(2,1)}, bf16[1,128,128]{2,1,0:T(8,128)(2,1)}, u32[]{:S(2)}, u32[]{:S(2)}) collective-permute-start(bf16[1,128,128]{2,1,0:T(8,128)(2,1)} %get-tuple-element.26), channel_id=1, source_target_pairs={{1,0},{3,2},{5,4},{7,6},{9,8},{11,10},{13,12},{15,14},{17,16},{19,... | collective-permute-start | bytes 98312 | tf_op jit(solution)/shard_map/ppermute | solution.py:18
  45.9 9.1 %collective-permute-start.4 = (bf16[1,128,128]{2,1,0:T(8,128)(2,1)}, bf16[1,128,128]{2,1,0:T(8,128)(2,1)S(1)}, u32[]{:S(2)}, u32[]{:S(2)}) collective-permute-start(bf16[1,128,128]{2,1,0:T(8,128)(2,1)} %get-tuple-element.25), channel_id=1, source_target_pairs={{0,1},{2,3},{4,5},{6,7},{8,9},{10,11},{12,13},{14,15},{16,17},{18,... | collective-permute-start | bytes 98312 | tf_op jit(solution)/shard_map/ppermute | solution.py:16
  62.3 9.8 %copy-start.1 = (bf16[8,128,9,128]{1,0,3,2:T(8,128)(2,1)S(1)}, bf16[8,128,9,128]{1,0,3,2:T(8,128)(2,1)}, u32[]{:S(2)}) copy-start(bf16[8,128,9,128]{1,0,3,2:T(8,128)(2,1)} %copy.26) | copy-start | bytes 7077892
  62.3 9.8 %copy-start.6 = (bf16[1,1,8,128,128]{4,3,2,1,0:T(8,128)(2,1)S(1)}, bf16[1,1,8,128,128]{4,3,2,1,0:T(8,128)(2,1)}, u32[]{:S(2)}) copy-start(bf16[1,1,8,128,128]{4,3,2,1,0:T(8,128)(2,1)} %get-tuple-element.17) | copy-start | bytes 786436
  65.7 10.2 %collective-permute-start.7 = (bf16[1,128,128]{2,1,0:T(8,128)(2,1)}, bf16[1,128,128]{2,1,0:T(8,128)(2,1)}, u32[]{:S(2)}, u32[]{:S(2)}) collective-permute-start(bf16[1,128,128]{2,1,0:T(8,128)(2,1)} %get-tuple-element.24), channel_id=1, source_target_pairs={{1,0},{3,2},{5,4},{7,6},{9,8},{11,10},{13,12},{15,14},{17,16},{19,... | collective-permute-start | bytes 98312 | tf_op jit(solution)/shard_map/ppermute | solution.py:18
  67.0 8.9 %collective-permute-start.6 = (bf16[1,128,128]{2,1,0:T(8,128)(2,1)}, bf16[1,128,128]{2,1,0:T(8,128)(2,1)S(1)}, u32[]{:S(2)}, u32[]{:S(2)}) collective-permute-start(bf16[1,128,128]{2,1,0:T(8,128)(2,1)} %get-tuple-element.23), channel_id=1, source_target_pairs={{0,1},{2,3},{4,5},{6,7},{8,9},{10,11},{12,13},{14,15},{16,17},{18,... | collective-permute-start | bytes 98312 | tf_op jit(solution)/shard_map/ppermute | solution.py:16
  78.1 2.7 %copy-start.5 = (bf16[1,1,8,128,128]{4,3,2,1,0:T(8,128)(2,1)S(1)}, bf16[1,1,8,128,128]{4,3,2,1,0:T(8,128)(2,1)}, u32[]{:S(2)}) copy-start(bf16[1,1,8,128,128]{4,3,2,1,0:T(8,128)(2,1)} %get-tuple-element.15) | copy-start | bytes 786436
  91.1 0.7 copy-start.9
  91.1 11.6 %copy-start.2 = (bf16[2,72,1152]{2,1,0:T(8,128)(2,1)S(1)}, bf16[2,72,1152]{2,1,0:T(8,128)(2,1)}, u32[]{:S(2)}) copy-start(bf16[2,72,1152]{2,1,0:T(8,128)(2,1)} %param.12) | copy-start | bytes 995332
  91.1 66.2 %copy-start.4 = (bf16[2,128,128]{2,1,0:T(8,128)(2,1)S(1)}, bf16[2,128,128]{2,1,0:T(8,128)(2,1)}, u32[]{:S(2)}) copy-start(bf16[2,128,128]{2,1,0:T(8,128)(2,1)} %param.13) | copy-start | bytes 196612
  91.1 100.9 %all-reduce.11.cloned.1.call-start = ((), (), s32[]{:S(2)}) async-start(), calls=%async_computation.4 | async-start | bytes 1474560 | tf_op jit(solution)/shard_map/psum | solution.py:83
  157.3 59.2 %all-reduce.9.cloned.1.call-start = ((), (), s32[]{:S(2)}) async-start(), calls=%async_computation.3 | async-start | bytes 262144 | tf_op jit(solution)/shard_map/psum | solution.py:27
  158.0 99.3 %all-gather.2.cloned.1.call-start = ((), (), s32[]{:S(2)}) async-start(), calls=%async_computation.2 | async-start | bytes 1253376 | tf_op jit(solution)/shard_map/all_gather | solution.py:100
  194.9 62.4 %copy-start.10 = (bf16[1,72,1152]{2,1,0:T(8,128)(2,1)S(1)}, bf16[1,72,1152]{2,1,0:T(8,128)(2,1)}, u32[]{:S(2)}) copy-start(bf16[1,72,1152]{2,1,0:T(8,128)(2,1)} %get-tuple-element.7) | copy-start | bytes 497668
  194.9 62.4 %copy-start.11 = (bf16[1,72,1152]{2,1,0:T(8,128)(2,1)S(1)}, bf16[1,72,1152]{2,1,0:T(8,128)(2,1)}, u32[]{:S(2)}) copy-start(bf16[1,72,1152]{2,1,0:T(8,128)(2,1)} %get-tuple-element.8) | copy-start | bytes 497668
  194.9 62.4 %copy-start.12 = (bf16[1,72,1152]{2,1,0:T(8,128)(2,1)S(1)}, bf16[1,72,1152]{2,1,0:T(8,128)(2,1)}, u32[]{:S(2)}) copy-start(bf16[1,72,1152]{2,1,0:T(8,128)(2,1)} %get-tuple-element.9) | copy-start | bytes 497668
  194.9 62.4 %copy-start.13 = (bf16[1,72,1152]{2,1,0:T(8,128)(2,1)S(1)}, bf16[1,72,1152]{2,1,0:T(8,128)(2,1)}, u32[]{:S(2)}) copy-start(bf16[1,72,1152]{2,1,0:T(8,128)(2,1)} %get-tuple-element.10) | copy-start | bytes 497668
Sparse Core Ops, SparseCore 0:
  91.2 64.3 reduce-scatter.1
  159.0 32.9 all-reduce.10
  194.6 21.8 all-reduce.8
  218.9 38.3 all-gather.1
where the time goes:
time: 268 us; the launch traced here: 266 us
  waiting for transfers between devices  146 us (54%)
  local copies, waits for them, and re-layouts  37.2 us (14%)
  starting transfers between devices  25.7 us (10%)
  between operations  24.6 us (9%)
  matrix products  20.3 us (8%)
  other arithmetic  12.4 us (5%)
    reduce_scatter x1, waiting for transfers between devices, per_device(): lax.psum_scatter(grad_term, 'dp', scatter_dimension=0, tiled=True)  52.2 us
    all_gather x1, waiting for transfers between devices, per_device(): gathered_piece = lax.all_gather(grad_sum, 'dp', axis=0, tiled=True)  40.8 us
    psum x1, waiting for transfers between devices, per_device(): grad_sum = lax.psum(grad_rows.astype(jnp.bfloat16), 'own')  34 us
    ppermute x4, starting transfers between devices, extended(): lax.ppermute(tail, axis, [(i, (i + 1) % count) for i in range(ends)])  20.4 us
    psum x1, waiting for transfers between devices, from_root(): return lax.psum(block, axis)  18.3 us
    another operation x11, local copies, waits for them, and re-layouts, tap_matrix(): stacked = jnp.stack(pieces, axis=2)  17.2 us
    dot_general x4, matrix products, per_device(): lax.dot_general(tap_rows, kernel, (((1,), (1,)), ((), ())), preferred_ele...  10.5 us
    mul x8, local copies, waits for them, and re-layouts, per_device(): grad_block.reshape(9 * channels, channels) * grad_scale  8.66 us
  transfers between devices with their start and end apart: 12, of which 5 were waited for; matrix products, arithmetic and copies ran while one was open for 8% of the time, Pallas kernels for 0%

commit v1 on v0

--- a/solution.py
+++ b/solution.py
@@ -24,7 +24,7 @@
 
 def from_root(block, axis, owner):
     block = jnp.where(lax.axis_index(axis) == owner, block, jnp.zeros_like(block))
-    return lax.psum(block, axis)
+    return jnp.sum(lax.all_gather(block, axis), axis=0)
 
 
 def loss_weight(labels):

time: 268 us -> 253 us (0.944)
  waiting for transfers between devices: 146 us -> 86.4 us
  blocking collectives: 0 us -> 42.8 us
    all_gather x0 -> x8, blocking collectives: none -> 42.8 us  [from_root(): return jnp.sum(lax.all_gather(block, axis), axis=0)]
    all_gather x1, waiting for transfers between devices: 40.8 us -> 0.01 us  [per_device(): gathered_piece = lax.all_gather(grad_sum, 'dp', axis=0, tiled=True)]
    psum x1 -> x0, waiting for transfers between devices: 18.3 us -> none  [from_root(): return lax.psum(block, axis)]
    psum x1, waiting for transfers between devices: 34 us -> 21 us  [per_device(): grad_sum = lax.psum(grad_rows.astype(jnp.bfloat16), 'own')]
    reduce_scatter x1, waiting for transfers between devices: 52.2 us -> 64.5 us  [per_device(): lax.psum_scatter(grad_term, 'dp', scatter_dimension=0, tiled=True)]
  transfers between devices with their start and end apart: 12 -> 11, of which waited for: 5 -> 3; matrix products, arithmetic and copies ran while one was open for 8% -> 9% of each run, Pallas kernels for 0% -> 0%
where the time goes in v1:
time: 253 us; the launch traced here: 251 us
  waiting for transfers between devices  86.4 us (34%)
  blocking collectives  42.8 us (17%)
  local copies, waits for them, and re-layouts  38.3 us (15%)
  starting transfers between devices  25.7 us (10%)
  between operations  24.9 us (10%)
  matrix products  19.1 us (8%)
  other arithmetic  14 us (6%)
    reduce_scatter x1, waiting for transfers between devices, per_device(): lax.psum_scatter(grad_term, 'dp', scatter_dimension=0, tiled=True)  64.5 us
    all_gather x8, blocking collectives, from_root(): return jnp.sum(lax.all_gather(block, axis), axis=0)  42.8 us
    psum x1, waiting for transfers between devices, per_device(): grad_sum = lax.psum(grad_rows.astype(jnp.bfloat16), 'own')  21 us
    ppermute x4, starting transfers between devices, extended(): lax.ppermute(tail, axis, [(i, (i + 1) % count) for i in range(ends)])  20.5 us
    another operation x11, local copies, waits for them, and re-layouts, tap_matrix(): stacked = jnp.stack(pieces, axis=2)  17.2 us
    dot_general x4, matrix products, per_device(): lax.dot_general(tap_rows, kernel, (((1,), (1,)), ((), ())), preferred_ele...  10.5 us
    mul x8, local copies, waits for them, and re-layouts, per_device(): grad_block.reshape(9 * channels, channels) * grad_scale  8.63 us
    dot_general x4, matrix products, per_device(): lax.dot_general(flat_inputs, tap_rows, (((0,), (0,)), ((), ())), preferre...  7.25 us
  transfers between devices with their start and end apart: 11, of which 3 were waited for; matrix products, arithmetic and copies ran while one was open for 9% of the time, Pallas kernels for 0%

profile of v1, /device:TPU:0, one launch (start us, length us, event | category | flops | bytes accessed | tf_op | source)
XLA Modules:
  0.0 251.3 jit_solution(16034031647148668245)
XLA Ops:
  10.5 4.8 %collective-permute-start = (bf16[1,128,128]{1,2,0:T(8,128)(2,1)S(1)}, bf16[1,128,128]{1,2,0:T(8,128)(2,1)S(1)}, u32[]{:S(2)}, u32[]{:S(2)}) collective-permute-start(bf16[1,128,128]{1,2,0:T(8,128)(2,1)S(1)} %get-tuple-element.20), channel_id=1, source_target_pairs={{0,1},{2,3},{4,5},{6,7},{8,9},{10,11},{12,13},{14,15},{16,17},{18,... | collective-permute-start | bytes 98312 | tf_op jit(solution)/shard_map/ppermute | solution.py:16
  21.5 1.6 copy.78
  23.1 1.8 fusion.13
  26.9 5.1 %collective-permute-start.2 = (bf16[1,128,128]{2,1,0:T(8,128)(2,1)}, bf16[1,128,128]{2,1,0:T(8,128)(2,1)S(1)}, u32[]{:S(2)}, u32[]{:S(2)}) collective-permute-start(bf16[1,128,128]{2,1,0:T(8,128)(2,1)} %get-tuple-element.18), channel_id=1, source_target_pairs={{0,1},{2,3},{4,5},{6,7},{8,9},{10,11},{12,13},{14,15},{16,17},{18,... | collective-permute-start | bytes 98312 | tf_op jit(solution)/shard_map/ppermute | solution.py:16
  36.1 2.6 %copy.76 = bf16[8,128,9,128]{1,0,3,2:T(8,128)(2,1)} copy(bf16[8,128,9,128]{3,1,0,2:T(8,128)(2,1)S(1)} %fusion.74) | data formatting | bytes 4718592 | tf_op jit(solution)/shard_map/stack | solution.py:41
  38.8 2.5 copy.68
  41.2 2.7 %fusion.14 = bf16[8,128,128]{2,1,0:T(8,128)(2,1)S(1)} fusion(bf16[8,128,1152]{1,2,0:T(8,128)(2,1)} %bitcast.253, bf16[128,1152,1]{1,0,2:T(8,128)(2,1)} %reshape.103, bf16[4,1,8,128,128]{4,3,2,1,0:T(8,128)(2,1)} %param.7), kind=kOutput, calls=%fused_computation.24 | convolution fusion | flops 302383104 | bytes 3178496 | tf_op jit(solution)/shard_map/dot_general | solution.py:70
  45.9 5.3 %collective-permute-start.4 = (bf16[1,128,128]{2,1,0:T(8,128)(2,1)}, bf16[1,128,128]{2,1,0:T(8,128)(2,1)S(1)}, u32[]{:S(2)}, u32[]{:S(2)}) collective-permute-start(bf16[1,128,128]{2,1,0:T(8,128)(2,1)} %get-tuple-element.16), channel_id=1, source_target_pairs={{0,1},{2,3},{4,5},{6,7},{8,9},{10,11},{12,13},{14,15},{16,17},{18,... | collective-permute-start | bytes 98312 | tf_op jit(solution)/shard_map/ppermute | solution.py:16
  51.2 1.6 fusion.2
  57.2 2.6 %copy.74 = bf16[8,128,9,128]{1,0,3,2:T(8,128)(2,1)} copy(bf16[8,128,9,128]{3,1,0,2:T(8,128)(2,1)S(1)} %fusion.64) | data formatting | bytes 4718592 | tf_op jit(solution)/shard_map/stack | solution.py:41
  59.9 2.5 copy.70
  62.4 2.7 %fusion.15 = bf16[8,128,128]{2,1,0:T(8,128)(2,1)S(1)} fusion(bf16[8,128,1152]{1,2,0:T(8,128)(2,1)} %bitcast.254, bf16[128,1152,1]{1,0,2:T(8,128)(2,1)} %reshape.104, bf16[4,1,8,128,128]{4,3,2,1,0:T(8,128)(2,1)} %param.7), kind=kOutput, calls=%fused_computation.25 | convolution fusion | flops 302383104 | bytes 3178496 | tf_op jit(solution)/shard_map/dot_general | solution.py:70
  67.0 5.1 %collective-permute-start.6 = (bf16[1,128,128]{2,1,0:T(8,128)(2,1)}, bf16[1,128,128]{2,1,0:T(8,128)(2,1)S(1)}, u32[]{:S(2)}, u32[]{:S(2)}) collective-permute-start(bf16[1,128,128]{2,1,0:T(8,128)(2,1)} %get-tuple-element.14), channel_id=1, source_target_pairs={{0,1},{2,3},{4,5},{6,7},{8,9},{10,11},{12,13},{14,15},{16,17},{18,... | collective-permute-start | bytes 98312 | tf_op jit(solution)/shard_map/ppermute | solution.py:16
  72.2 1.6 fusion.1
  78.2 2.6 %copy.72 = bf16[8,128,9,128]{1,0,3,2:T(8,128)(2,1)} copy(bf16[8,128,9,128]{3,1,0,2:T(8,128)(2,1)S(1)} %fusion.54) | data formatting | bytes 4718592 | tf_op jit(solution)/shard_map/stack | solution.py:41
  80.8 3.3 %fusion = f32[128,1152]{0,1:T(8,128)} fusion(bf16[1024,128]{1,0:T(8,128)(2,1)S(1)} %bitcast.257, bf16[144,8,8,128]{3,2,1,0:T(8,128)(2,1)} %bitcast.255), kind=kOutput, calls=%fused_computation.4 | convolution fusion | flops 302137344 | bytes 3211264 | tf_op jit(solution)/shard_map/dot_general | solution.py:65
  84.1 2.1 copy.73
  86.2 1.9 mul.59
  88.1 3.0 %pad_maximum_fusion = f32[1152,512]{1,0:T(8,128)} fusion(f32[1152,128]{1,0:T(8,128)S(1)} %mul.68, f32[1152,128]{1,0:T(8,128)} %mul.65, f32[1152,128]{1,0:T(8,128)} %mul.62, f32[1152,128]{1,0:T(8,128)} %mul.59), kind=kLoop, calls=%fused_computation.16 | loop fusion | flops 1769472 | bytes 4718592 | tf_op jit(solution)/shard_map/concatenate | solution.py:80
  91.2 64.5 %reduce-scatter.2.cloned.1.call-done = f32[72,512]{1,0:T(8,128)} async-done(((f32[1152,512]{1,0:T(8,128)}), f32[72,512]{1,0:T(8,128)}) %reduce-scatter.2.cloned.1.call-update) | async-done | bytes 147472 | tf_op jit(solution)/shard_map/reduce_scatter | solution.py:81
  157.3 21.0 %all-reduce.6.cloned.1.call-done = bf16[72,512]{1,0:T(8,128)(2,1)} async-done(((bf16[72,512]{1,0:T(8,128)(2,1)}), bf16[72,512]{1,0:T(8,128)(2,1)}) %all-reduce.6.cloned.1.call-update) | async-done | bytes 73744 | tf_op jit(solution)/shard_map/psum | solution.py:83
  189.7 6.4 %all_gather.38 = bf16[2,72,1152]{2,1,0:T(8,128)(2,1)S(1)} all-gather(bf16[1,72,1152]{2,1,0:T(8,128)(2,1)S(1)} %get-tuple-element.12), channel_id=1, replica_groups=mesh['dp'=16,'own'=2] {'own'}, dimensions={0}, use_global_device_ids=true | all-gather | bytes 497664 | tf_op jit(solution)/shard_map/all_gather | solution.py:27
  196.8 6.0 %all_gather.37 = bf16[2,72,1152]{2,1,0:T(8,128)(2,1)S(1)} all-gather(bf16[1,72,1152]{2,1,0:T(8,128)(2,1)S(1)} %get-tuple-element.13), channel_id=1, replica_groups=mesh['dp'=16,'own'=2] {'own'}, dimensions={0}, use_global_device_ids=true | all-gather | bytes 497664 | tf_op jit(solution)/shard_map/all_gather | solution.py:27
  202.9 6.0 %all_gather.36 = bf16[2,72,1152]{2,1,0:T(8,128)(2,1)S(1)} all-gather(bf16[1,72,1152]{2,1,0:T(8,128)(2,1)S(1)} %get-tuple-element.11), channel_id=1, replica_groups=mesh['dp'=16,'own'=2] {'own'}, dimensions={0}, use_global_device_ids=true | all-gather | bytes 497664 | tf_op jit(solution)/shard_map/all_gather | solution.py:27
  209.0 6.0 %all_gather.35 = bf16[2,72,1152]{2,1,0:T(8,128)(2,1)S(1)} all-gather(bf16[1,72,1152]{2,1,0:T(8,128)(2,1)S(1)} %get-tuple-element.10), channel_id=1, replica_groups=mesh['dp'=16,'own'=2] {'own'}, dimensions={0}, use_global_device_ids=true | all-gather | bytes 497664 | tf_op jit(solution)/shard_map/all_gather | solution.py:27
  216.0 4.6 %all_gather.43 = bf16[2,128,128]{2,1,0:T(8,128)(2,1)S(1)} all-gather(bf16[1,128,128]{2,1,0:T(8,128)(2,1)S(1)} %get-tuple-element.24), channel_id=1, replica_groups=mesh['dp'=16,'own'=2] {'own'}, dimensions={0}, use_global_device_ids=true | all-gather | bytes 98304 | tf_op jit(solution)/shard_map/all_gather | solution.py:27
  220.6 4.6 %all_gather.42 = bf16[2,128,128]{2,1,0:T(8,128)(2,1)S(1)} all-gather(bf16[1,128,128]{2,1,0:T(8,128)(2,1)S(1)} %get-tuple-element.25), channel_id=1, replica_groups=mesh['dp'=16,'own'=2] {'own'}, dimensions={0}, use_global_device_ids=true | all-gather | bytes 98304 | tf_op jit(solution)/shard_map/all_gather | solution.py:27
  225.2 4.6 %all_gather.41 = bf16[2,128,128]{2,1,0:T(8,128)(2,1)S(1)} all-gather(bf16[1,128,128]{2,1,0:T(8,128)(2,1)S(1)} %get-tuple-element.23), channel_id=1, replica_groups=mesh['dp'=16,'own'=2] {'own'}, dimensions={0}, use_global_device_ids=true | all-gather | bytes 98304 | tf_op jit(solution)/shard_map/all_gather | solution.py:27
  230.4 4.6 %all_gather.40 = bf16[2,128,128]{2,1,0:T(8,128)(2,1)S(1)} all-gather(bf16[1,128,128]{2,1,0:T(8,128)(2,1)S(1)} %get-tuple-element.22), channel_id=1, replica_groups=mesh['dp'=16,'own'=2] {'own'}, dimensions={0}, use_global_device_ids=true | all-gather | bytes 98304 | tf_op jit(solution)/shard_map/all_gather | solution.py:27
  236.0 2.5 copy.82
  238.4 3.2 %fusion.16 = bf16[1,8,128,128]{3,2,1,0:T(8,128)(2,1)} fusion(bf16[8,128,1152]{1,2,0:T(8,128)(2,1)} %bitcast.248, bf16[128,1152,1]{1,0,2:T(8,128)(2,1)S(1)} %reshape.105), kind=kOutput, calls=%fused_computation.27 | convolution fusion | flops 302120960 | bytes 2916352 | tf_op jit(solution)/shard_map/dot_general | solution.py:70
  241.7 1.7 copy.80
  (116 shorter events, 34.9 us)
Async XLA Ops:
  7.2 9.5 %copy-start.3 = (bf16[4,1,8,128,128]{4,3,2,1,0:T(8,128)(2,1)S(1)}, bf16[4,1,8,128,128]{4,3,2,1,0:T(8,128)(2,1)}, u32[]{:S(2)}) copy-start(bf16[4,1,8,128,128]{4,3,2,1,0:T(8,128)(2,1)} %param.7) | copy-start | bytes 3145732
  7.2 148.5 %reduce-scatter.2.cloned.1.call-start = ((), (), s32[]{:S(2)}) async-start(), calls=%async_computation.1 | async-start | bytes 2506752 | tf_op jit(solution)/shard_map/reduce_scatter | solution.py:81
  9.2 11.0 %collective-permute-start.1 = (bf16[1,128,128]{1,2,0:T(8,128)(2,1)S(1)}, bf16[1,128,128]{1,2,0:T(8,128)(2,1)S(1)}, u32[]{:S(2)}, u32[]{:S(2)}) collective-permute-start(bf16[1,128,128]{1,2,0:T(8,128)(2,1)S(1)} %get-tuple-element.21), channel_id=1, source_target_pairs={{1,0},{3,2},{5,4},{7,6},{9,8},{11,10},{13,12},{15,14},{17,16},{19,... | collective-permute-start | bytes 98312 | tf_op jit(solution)/shard_map/ppermute | solution.py:18
  10.5 9.7 %collective-permute-start = (bf16[1,128,128]{1,2,0:T(8,128)(2,1)S(1)}, bf16[1,128,128]{1,2,0:T(8,128)(2,1)S(1)}, u32[]{:S(2)}, u32[]{:S(2)}) collective-permute-start(bf16[1,128,128]{1,2,0:T(8,128)(2,1)S(1)} %get-tuple-element.20), channel_id=1, source_target_pairs={{0,1},{2,3},{4,5},{6,7},{8,9},{10,11},{12,13},{14,15},{16,17},{18,... | collective-permute-start | bytes 98312 | tf_op jit(solution)/shard_map/ppermute | solution.py:16
  23.1 8.9 %copy-start.7 = (bf16[1,1,8,128,128]{4,3,2,1,0:T(8,128)(2,1)S(1)}, bf16[1,1,8,128,128]{4,3,2,1,0:T(8,128)(2,1)}, u32[]{:S(2)}) copy-start(bf16[1,1,8,128,128]{4,3,2,1,0:T(8,128)(2,1)} %get-tuple-element.9) | copy-start | bytes 786436
  25.6 7.5 %collective-permute-start.3 = (bf16[1,128,128]{2,1,0:T(8,128)(2,1)}, bf16[1,128,128]{2,1,0:T(8,128)(2,1)}, u32[]{:S(2)}, u32[]{:S(2)}) collective-permute-start(bf16[1,128,128]{2,1,0:T(8,128)(2,1)} %get-tuple-element.19), channel_id=1, source_target_pairs={{1,0},{3,2},{5,4},{7,6},{9,8},{11,10},{13,12},{15,14},{17,16},{19,... | collective-permute-start | bytes 98312 | tf_op jit(solution)/shard_map/ppermute | solution.py:18
  26.9 7.0 %collective-permute-start.2 = (bf16[1,128,128]{2,1,0:T(8,128)(2,1)}, bf16[1,128,128]{2,1,0:T(8,128)(2,1)S(1)}, u32[]{:S(2)}, u32[]{:S(2)}) collective-permute-start(bf16[1,128,128]{2,1,0:T(8,128)(2,1)} %get-tuple-element.18), channel_id=1, source_target_pairs={{0,1},{2,3},{4,5},{6,7},{8,9},{10,11},{12,13},{14,15},{16,17},{18,... | collective-permute-start | bytes 98312 | tf_op jit(solution)/shard_map/ppermute | solution.py:16
  41.2 10.0 %copy-start = (bf16[8,128,9,128]{1,0,3,2:T(8,128)(2,1)S(1)}, bf16[8,128,9,128]{1,0,3,2:T(8,128)(2,1)}, u32[]{:S(2)}) copy-start(bf16[8,128,9,128]{1,0,3,2:T(8,128)(2,1)} %copy.76) | copy-start | bytes 7077892
  41.2 10.0 %copy-start.6 = (bf16[1,1,8,128,128]{4,3,2,1,0:T(8,128)(2,1)S(1)}, bf16[1,1,8,128,128]{4,3,2,1,0:T(8,128)(2,1)}, u32[]{:S(2)}) copy-start(bf16[1,1,8,128,128]{4,3,2,1,0:T(8,128)(2,1)} %get-tuple-element.7) | copy-start | bytes 786436
  44.6 10.4 %collective-permute-start.5 = (bf16[1,128,128]{2,1,0:T(8,128)(2,1)}, bf16[1,128,128]{2,1,0:T(8,128)(2,1)}, u32[]{:S(2)}, u32[]{:S(2)}) collective-permute-start(bf16[1,128,128]{2,1,0:T(8,128)(2,1)} %get-tuple-element.17), channel_id=1, source_target_pairs={{1,0},{3,2},{5,4},{7,6},{9,8},{11,10},{13,12},{15,14},{17,16},{19,... | collective-permute-start | bytes 98312 | tf_op jit(solution)/shard_map/ppermute | solution.py:18
  45.9 9.1 %collective-permute-start.4 = (bf16[1,128,128]{2,1,0:T(8,128)(2,1)}, bf16[1,128,128]{2,1,0:T(8,128)(2,1)S(1)}, u32[]{:S(2)}, u32[]{:S(2)}) collective-permute-start(bf16[1,128,128]{2,1,0:T(8,128)(2,1)} %get-tuple-element.16), channel_id=1, source_target_pairs={{0,1},{2,3},{4,5},{6,7},{8,9},{10,11},{12,13},{14,15},{16,17},{18,... | collective-permute-start | bytes 98312 | tf_op jit(solution)/shard_map/ppermute | solution.py:16
  62.3 9.8 %copy-start.1 = (bf16[8,128,9,128]{1,0,3,2:T(8,128)(2,1)S(1)}, bf16[8,128,9,128]{1,0,3,2:T(8,128)(2,1)}, u32[]{:S(2)}) copy-start(bf16[8,128,9,128]{1,0,3,2:T(8,128)(2,1)} %copy.74) | copy-start | bytes 7077892
  62.4 9.8 %copy-start.5 = (bf16[1,1,8,128,128]{4,3,2,1,0:T(8,128)(2,1)S(1)}, bf16[1,1,8,128,128]{4,3,2,1,0:T(8,128)(2,1)}, u32[]{:S(2)}) copy-start(bf16[1,1,8,128,128]{4,3,2,1,0:T(8,128)(2,1)} %get-tuple-element.8) | copy-start | bytes 786436
  65.7 10.2 %collective-permute-start.7 = (bf16[1,128,128]{2,1,0:T(8,128)(2,1)}, bf16[1,128,128]{2,1,0:T(8,128)(2,1)}, u32[]{:S(2)}, u32[]{:S(2)}) collective-permute-start(bf16[1,128,128]{2,1,0:T(8,128)(2,1)} %get-tuple-element.15), channel_id=1, source_target_pairs={{1,0},{3,2},{5,4},{7,6},{9,8},{11,10},{13,12},{15,14},{17,16},{19,... | collective-permute-start | bytes 98312 | tf_op jit(solution)/shard_map/ppermute | solution.py:18
  67.0 8.9 %collective-permute-start.6 = (bf16[1,128,128]{2,1,0:T(8,128)(2,1)}, bf16[1,128,128]{2,1,0:T(8,128)(2,1)S(1)}, u32[]{:S(2)}, u32[]{:S(2)}) collective-permute-start(bf16[1,128,128]{2,1,0:T(8,128)(2,1)} %get-tuple-element.14), channel_id=1, source_target_pairs={{0,1},{2,3},{4,5},{6,7},{8,9},{10,11},{12,13},{14,15},{16,17},{18,... | collective-permute-start | bytes 98312 | tf_op jit(solution)/shard_map/ppermute | solution.py:16
  78.1 2.7 %copy-start.4 = (bf16[1,1,8,128,128]{4,3,2,1,0:T(8,128)(2,1)S(1)}, bf16[1,1,8,128,128]{4,3,2,1,0:T(8,128)(2,1)}, u32[]{:S(2)}) copy-start(bf16[1,1,8,128,128]{4,3,2,1,0:T(8,128)(2,1)} %get-tuple-element.6) | copy-start | bytes 786436
  91.1 87.2 %copy-start.11 = (s32[4]{0:T(128)S(1)}, s32[4]{0:T(128)}, u32[]{:S(2)}) copy-start(s32[4]{0:T(128)} %param.11) | copy-start | bytes 52
  91.1 98.5 %copy-start.2 = (bf16[2,72,1152]{2,1,0:T(8,128)(2,1)S(1)}, bf16[2,72,1152]{2,1,0:T(8,128)(2,1)}, u32[]{:S(2)}) copy-start(bf16[2,72,1152]{2,1,0:T(8,128)(2,1)} %param.12) | copy-start | bytes 995332
  91.1 87.2 %all-reduce.6.cloned.1.call-start = ((), (), s32[]{:S(2)}) async-start(), calls=%async_computation.2 | async-start | bytes 147456 | tf_op jit(solution)/shard_map/psum | solution.py:83
  157.3 84.4 %all-gather.2.cloned.1.call-start = ((), (), s32[]{:S(2)}) async-start(), calls=%async_computation.3 | async-start | bytes 1253376 | tf_op jit(solution)/shard_map/all_gather | solution.py:100
  238.4 4.9 %copy-start.8 = (bf16[72,1152]{1,0:T(8,128)(2,1)S(1)}, bf16[72,1152]{1,0:T(8,128)(2,1)}, u32[]{:S(2)}) copy-start(bf16[72,1152]{1,0:T(8,128)(2,1)} %reduce_sum.99) | copy-start | bytes 497668
  238.4 4.9 %copy-start.9 = (bf16[128,128]{1,0:T(8,128)(2,1)S(1)}, bf16[128,128]{1,0:T(8,128)(2,1)}, u32[]{:S(2)}) copy-start(bf16[128,128]{1,0:T(8,128)(2,1)} %reduce_sum.101) | copy-start | bytes 98308
  238.4 4.9 %copy-start.10 = (bf16[128,128]{1,0:T(8,128)(2,1)S(1)}, bf16[128,128]{1,0:T(8,128)(2,1)}, u32[]{:S(2)}) copy-start(bf16[128,128]{1,0:T(8,128)(2,1)} %reduce_sum.100) | copy-start | bytes 98308
Sparse Core Ops, SparseCore 0:
  91.2 64.4 reduce-scatter.1
  158.6 19.6 all-reduce.5
  180.9 38.5 all-gather.1
